TPU v7x, 32 devices: a whole 2x2x4 slice. The times are simulated.
32 devices in a mesh: hi: 4 (over z), lo: 8 (over y, x, core).
Axes of the slice: x: 2, y: 2, z: 4, core: 2. Of those that a mesh axis runs over, the one named last changes fastest.
Arguments:
- ket_state: float32 [2, 2097152], P(None, ('hi', 'lo')), may hold values from -6 to 6
- bra_state: float32 [2, 2097152], P(None, ('hi', 'lo')), may hold values from -6 to 6
- gates: float32 [4, 4, 2, 128, 128], replicated, may hold values from -0.375 to 0.375
- targets: int32 [4, 4, 128], replicated, may hold values from 0 to 127, each once within a row
- swap_order: int32 [4, 8], replicated, may hold values from 0 to 7, each once within a row
Outputs:
- ket_final: float32 [2, 2097152], P(None, ('hi', 'lo'))
- bra_final: float32 [2, 2097152], P(None, ('hi', 'lo'))
- gate_grads: float32 [4, 4, 2, 128, 128], P(None, None, None, 'hi')
Inputs may be any that keep to these rules, and one draw needn't show every extreme that they name: Each row of targets holds every value once. Each row of swap_order holds every value once.
All inputs are finite; a program needn't handle non-finite values.
Results may differ from a plain program's by a relative error of at most 0.00015.
Values sent between devices are 32-bit elements; how exact they have to be, the bound alone decides.
A program may use at most 64 MiB of HBM per device.

v0:
```python
import functools

import jax
import jax.numpy as jnp
from jax import lax
from jax.experimental import pallas as pl
from jax.experimental.pallas import tpu as pltpu
from jax.sharding import PartitionSpec as P

bf16 = jnp.bfloat16
f32 = jnp.float32


def split(x):
    high = x.astype(bf16)
    return high, (x - high.astype(f32)).astype(bf16)


def mm(a, b):
    return lax.dot_general(a, b, (((1,), (0,)), ((), ())), preferred_element_type=f32)


def mm_nt(a, b):
    return lax.dot_general(a, b, (((1,), (1,)), ((), ())), preferred_element_type=f32)


def block_swap(x):
    r, c = x.shape[0] // 2, x.shape[1] // 2
    return jnp.concatenate(
        [
            jnp.concatenate([x[:r, :c], x[r:, :c]], axis=1),
            jnp.concatenate([x[:r, c:], x[r:, c:]], axis=1),
        ],
        axis=0,
    )


def kernel(
    n_hi, n_lo, layers, gate_count, chunks, width, scale,
    sigma_ref, ket_ref, bra_ref, gates_hbm, targets_ref, ket_out, bra_out, grad_hbm,
    rbuf, sbuf, ybuf, vbuf, acc, r0buf, hsum, r1buf, p1, r2buf, gout,
    gates_ref, gates_sem, gather_s, gather_r, trade_s, trade_r, home_s, home_r, s0, q0, s1, q1, s2, q2, s3, q3, gsem,
):
    h = lax.axis_index("hi")
    q = lax.axis_index("lo")
    core = lax.rem(q, 2)
    chip = q // 2
    n_chip = n_lo // 2
    half = gate_count // 2
    rows = width // n_hi
    piece = rows // n_chip

    def lo_peer(k):
        return lax.rem(q + k, n_lo)

    def hi_peer(k):
        return lax.rem(h + k, n_hi)

    def chip_peer(k):
        return lax.rem(chip + k, n_chip)

    gates_copy = pltpu.make_async_copy(gates_hbm, gates_ref, gates_sem)
    gates_copy.start()

    def entering(m):
        parts = [
            jnp.concatenate(
                [v[pl.ds(2 * m + c, width, stride=2 * chunks), :] for v in (ket_ref, bra_ref)], axis=1
            )
            for c in range(2)
        ]
        return jnp.concatenate(parts, axis=0)

    barrier = pltpu.get_barrier_semaphore()
    for k in range(1, n_lo):
        pl.semaphore_signal(barrier, inc=1, device_id={"lo": lo_peer(k)})
    for k in range(1, n_hi):
        pl.semaphore_signal(barrier, inc=1, device_id={"hi": hi_peer(k)})

    def prepare(layer, gate):
        order = targets_ref[layer, gate]
        picks = (
            jnp.broadcast_to(order, (width, width))
            == lax.broadcasted_iota(jnp.int32, (width, width), 0)
        ).astype(f32)
        rows_pick = picks.T.astype(bf16)
        g = gates_ref[layer, gate]
        rh, rl = split(g[0])
        ih, il = split(g[1])
        t = mm(jnp.concatenate([rh, ih, rl, il], axis=0), picks.astype(bf16)).astype(bf16)
        w = mm(
            rows_pick,
            jnp.concatenate([t[i * width:(i + 1) * width] for i in range(4)], axis=1),
        ).astype(bf16)
        wrh, wih, wrl, wil = [w[:, i * width:(i + 1) * width] for i in range(4)]
        vbuf[layer, gate] = jnp.concatenate(
            [
                jnp.concatenate([wrh, -wih, wrh, -wih, wrl, -wil], axis=1),
                jnp.concatenate([wih, wrh, wih, wrh, wil, wrl], axis=1),
            ],
            axis=0,
        )

    gates_copy.wait()
    for g in range(gate_count):
        prepare(0, g)
    acc[...] = jnp.zeros_like(acc)
    pl.semaphore_wait(barrier, n_lo - 1 + n_hi - 1)

    def gather_copy(kc, ke, incoming=False):
        m, e = chip_peer(kc), lax.rem(core + ke, 2)
        d = 2 * m + e
        return pltpu.make_async_remote_copy(
            src_ref=sbuf.at[0, m, pl.ds(chunks * e, chunks)],
            dst_ref=rbuf.at[1, :, :, d if incoming else q],
            send_sem=gather_s.at[d],
            recv_sem=gather_r.at[d if incoming else q],
            device_id={"lo": d},
        )

    def trade_copy(l, i, incoming=False):
        return pltpu.make_async_remote_copy(
            src_ref=sbuf.at[l, i, pl.ds(0, chunks)],
            dst_ref=rbuf.at[l + 1, :, :, 2 * i + (1 - core if incoming else core)],
            send_sem=trade_s.at[l, i],
            recv_sem=trade_r.at[l, i],
            device_id={"lo": q + 1 - 2 * core},
        )

    def home_copy(i, kc, ke, incoming=False):
        m, e = chip_peer(kc), lax.rem(core + ke, 2)
        d = 2 * m + e
        return pltpu.make_async_remote_copy(
            src_ref=sbuf.at[last, i, d],
            dst_ref=rbuf.at[layers, m if incoming else chip, :, 2 * i + (e if incoming else core)],
            send_sem=home_s.at[i, d],
            recv_sem=home_r.at[i, d if incoming else q],
            device_id={"lo": d},
        )

    last = layers - 1
    chip_order = [k for k in range(n_chip) if k % 2] + list(range(2, n_chip, 2)) + [0]
    targets_order = [(kc, ke) for kc in chip_order for ke in (1, 0)]
    others = [pair for pair in targets_order if pair != (0, 0)]

    def r0_copy(l):
        return pltpu.make_async_remote_copy(
            src_ref=acc.at[l, pl.ds(half * (1 - core), half)],
            dst_ref=r0buf.at[l],
            send_sem=s0.at[l],
            recv_sem=q0.at[l],
            device_id={"lo": q + 1 - 2 * core},
        )

    def r1_copy(l, k, incoming=False):
        d = hi_peer(k)
        return pltpu.make_async_remote_copy(
            src_ref=hsum.at[l, :, :, d],
            dst_ref=r1buf.at[l, d if incoming else h],
            send_sem=s1.at[l, d],
            recv_sem=q1.at[l, d if incoming else h],
            device_id={"hi": d},
        )

    def r2_copy(l, k, incoming=False):
        d = chip_peer(k)
        return pltpu.make_async_remote_copy(
            src_ref=p1.at[l, :, :, d],
            dst_ref=r2buf.at[l, d if incoming else chip],
            send_sem=s2.at[l, d],
            recv_sem=q2.at[l, d if incoming else chip],
            device_id={"lo": 2 * d + core},
        )

    def r3_copy(l, k, incoming=False):
        d = lo_peer(k)
        owner = d if incoming else q
        place = gout.at[l, pl.ds(half * lax.rem(owner, 2), half), :, owner // 2]
        return pltpu.make_async_remote_copy(
            src_ref=place,
            dst_ref=place,
            send_sem=s3.at[l, d],
            recv_sem=q3.at[l, owner],
            device_id={"lo": d},
        )

    def stage0(l):
        r0_copy(l).wait_recv()
        total = acc[l, pl.ds(half * core, half)] + r0buf[l]
        hsum[l] = total.reshape(half, 2, n_hi, rows, width)
        for k in range(1, n_hi):
            r1_copy(l, k).start()

    def stage1(l):
        total = hsum[l, :, :, h]
        for k in range(1, n_hi):
            r1_copy(l, k, True).wait_recv()
            total = total + r1buf[l, hi_peer(k)]
        p1[l] = total.reshape(half, 2, n_chip, piece, width)
        for k in range(1, n_chip):
            r2_copy(l, k).start()

    def stage2(l):
        total = p1[l, :, :, chip]
        for k in range(1, n_chip):
            r2_copy(l, k, True).wait_recv()
            total = total + r2buf[l, chip_peer(k)]
        gout[l, pl.ds(half * core, half), :, chip] = total * scale
        for k in range(1, n_lo):
            r3_copy(l, k).start()

    def cat(v, axis):
        return jnp.concatenate(v, axis=axis) if len(v) > 1 else v[0]

    def run_gates(ss, l):
        n = len(ss)
        w2 = 2 * width
        hs, ls = zip(*[split(s) for s in ss])
        for g in range(gate_count):
            v = vbuf[l, g]
            if g % 2 == 0:
                xh = cat([block_swap(t) for t in hs], 0)
                xl = cat([block_swap(t) for t in ls], 0)
                y = mm_nt(cat([xh, xl, xh], 1), v)
                ys = [y[i * w2:(i + 1) * w2] for i in range(n)]
                yhs, yls = zip(*[split(t) for t in ys])
                bt = cat([cat([s[:width, width:], s[width:, width:]], 1).T for s in ss], 1)
                bh, bl = split(bt)
                kh, kl = cat([t[:width] for t in yhs], 0), cat([t[:width] for t in yls], 0)
                grad = mm(cat([bh, bh, bl], 1), cat([kh, kl, kh], 0))
                ss = [block_swap(t) for t in ys]
                hs = [block_swap(t) for t in yhs]
                ls = [block_swap(t) for t in yls]
            else:
                sh, sl = cat(hs, 1), cat(ls, 1)
                y = mm(v, cat([sh, sl, sh], 0))
                ys = [y[:, i * w2:(i + 1) * w2] for i in range(n)]
                yhs, yls = zip(*[split(t) for t in ys])
                bh, bl = cat([t[:, width:] for t in hs], 1), cat([t[:, width:] for t in ls], 1)
                kh, kl = cat([t[:, :width] for t in yhs], 1), cat([t[:, :width] for t in yls], 1)
                grad = mm_nt(cat([bh, bh, bl], 1), cat([kh, kl, kh], 1))
                ss, hs, ls = ys, yhs, yls
            acc[l, g, 0] += grad[:width, :width] + grad[width:, width:]
            acc[l, g, 1] += grad[width:, :width] - grad[:width, width:]
        return ss

    def load(l, i):
        return rbuf[l, i].reshape(2 * width, 2 * width)

    for first in range(0, chunks, 2):
        todo = chip_order[first:first + 2]
        states = run_gates([entering(chip_peer(kc)) for kc in todo], 0)
        for kc, state in zip(todo, states):
            m = chip_peer(kc)
            ybuf[kc] = state.reshape(ybuf.shape[1:])
            for ke in (1, 0):
                e = lax.rem(core + ke, 2)
                for j in range(chunks):
                    block = ybuf[kc, :, sigma_ref[0, 2 * j + e]]
                    if (kc, ke) == (0, 0):
                        rbuf[1, j, :, q] = block
                    else:
                        sbuf[0, m, chunks * e + j] = block
                if (kc, ke) != (0, 0):
                    gather_copy(kc, ke).start()
    r0_copy(0).start()

    @pl.loop(1, layers)
    def _(l):
        @pl.loop(0, gate_count)
        def _(g):
            prepare(l, g)

    stage0(0)
    for kc, ke in others:
        gather_copy(kc, ke, True).wait_recv()

    def middle(l):
        states = run_gates([load(l, i) for i in range(chunks)], l)
        for i, state in enumerate(states):
            ybuf[i] = state.reshape(ybuf.shape[1:])
            for j in range(chunks):
                sbuf[l, i, j] = ybuf[i, :, sigma_ref[l, 2 * j + 1 - core]]
            trade_copy(l, i).start()
            for j in range(chunks):
                rbuf[l + 1, j, :, 2 * i + core] = ybuf[i, :, sigma_ref[l, 2 * j + core]]
        r0_copy(l).start()

    @pl.loop(1, last)
    def _(l):
        middle(l)

        @pl.when(l == 1)
        def _():
            stage1(0)

        @pl.when(l > 2)
        def _():
            stage1(l - 2)

        @pl.when(l > 1)
        def _():
            stage2(l - 2)
            stage0(l - 1)

        for i in range(chunks):
            trade_copy(l, i, True).wait_recv()

    for first in range(0, chunks, 2):
        states = run_gates([load(last, first + i) for i in range(2)], last)
        for i, state in enumerate(states):
            i = first + i
            ybuf[i] = state.reshape(ybuf.shape[1:])
            for kc, ke in targets_order:
                d = 2 * chip_peer(kc) + lax.rem(core + ke, 2)
                block = ybuf[i, :, sigma_ref[last, d]]
                if (kc, ke) == (0, 0):
                    rbuf[layers, chip, :, 2 * i + core] = block
                else:
                    sbuf[last, i, d] = block
                    home_copy(i, kc, ke).start()
        if first == 0:
            stage0(last - 1)
    r0_copy(last).start()
    stage1(last - 2)
    stage0(last)
    stage1(last - 1)
    stage2(last - 2)
    stage1(last)
    stage2(last - 1)
    stage2(last)

    for kc in [0] + [k for k in chip_order if k]:
        for ke in (1, 0):
            if (kc, ke) != (0, 0):
                for i in range(chunks):
                    home_copy(i, kc, ke, True).wait_recv()
        m = chip_peer(kc)
        state = load(layers, m)
        for c in range(2):
            for n, out in enumerate((ket_out, bra_out)):
                out[pl.ds(2 * m + c, width, stride=2 * chunks), :] = state[
                    c * width:(c + 1) * width, n * width:(n + 1) * width
                ]

    @pl.loop(0, layers)
    def _(l):
        for k in range(1, n_lo):
            r3_copy(l, k, True).wait_recv()

    grads = pltpu.make_async_copy(gout, grad_hbm, gsem)
    grads.start()

    for kc, ke in others:
        gather_copy(kc, ke).wait_send()

    @pl.loop(0, chunks)
    def _(i):
        for kc, ke in others:
            home_copy(i, kc, ke).wait_send()

        @pl.loop(1, last)
        def _(l):
            trade_copy(l, i).wait_send()

    @pl.loop(0, layers)
    def _(l):
        r0_copy(l).wait_send()
        for k in range(1, n_hi):
            r1_copy(l, k).wait_send()
        for k in range(1, n_chip):
            r2_copy(l, k).wait_send()
        for k in range(1, n_lo):
            r3_copy(l, k).wait_send()

    grads.wait()


def fast_body(ket_state, bra_state, gates, targets, swap_order):
    layers, gate_count, _, width, _ = gates.shape
    n_lo, n_hi = lax.axis_size("lo"), lax.axis_size("hi")
    amps = ket_state.shape[1]
    chunks = amps // (width * width)
    unit = width // n_lo
    half = gate_count // 2
    n_chip = n_lo // 2
    rows = width // n_hi
    piece = rows // n_chip
    scale = (amps * n_lo * n_hi // width) ** (-0.5)
    shape = (chunks, 2, n_lo, unit, 2 * width)

    def as_rows(v):
        return v.reshape(2, amps // width, width).transpose(1, 0, 2).reshape(-1, width)

    def from_rows(v):
        return v.reshape(amps // width, 2, width).transpose(1, 0, 2).reshape(2, amps)

    dma = pltpu.SemaphoreType.DMA
    ket_out, bra_out, grads = pl.pallas_call(
        functools.partial(kernel, n_hi, n_lo, layers, gate_count, chunks, width, scale),
        out_shape=(
            jax.ShapeDtypeStruct((2 * amps // width, width), f32),
            jax.ShapeDtypeStruct((2 * amps // width, width), f32),
            jax.ShapeDtypeStruct((layers, gate_count, 2, n_chip, piece, width), f32),
        ),
        in_specs=[
            pl.BlockSpec(memory_space=pltpu.SMEM),
            pl.BlockSpec(memory_space=pltpu.VMEM),
            pl.BlockSpec(memory_space=pltpu.VMEM),
            pl.BlockSpec(memory_space=pl.ANY),
            pl.BlockSpec(memory_space=pltpu.VMEM),
        ],
        out_specs=[
            pl.BlockSpec(memory_space=pltpu.VMEM),
            pl.BlockSpec(memory_space=pltpu.VMEM),
            pl.BlockSpec(memory_space=pl.ANY),
        ],
        scratch_shapes=[
            pltpu.VMEM((layers + 1,) + shape, f32),
            pltpu.VMEM((layers, chunks, n_lo, 2, unit, 2 * width), f32),
            pltpu.VMEM(shape, f32),
            pltpu.VMEM((layers, gate_count, 2 * width, 6 * width), bf16),
            pltpu.VMEM((layers, gate_count, 2, width, width), f32),
            pltpu.VMEM((layers, half, 2, width, width), f32),
            pltpu.VMEM((layers, half, 2, n_hi, rows, width), f32),
            pltpu.VMEM((layers, n_hi, half, 2, rows, width), f32),
            pltpu.VMEM((layers, half, 2, n_chip, piece, width), f32),
            pltpu.VMEM((layers, n_chip, half, 2, piece, width), f32),
            pltpu.VMEM((layers, gate_count, 2, n_chip, piece, width), f32),
            pltpu.VMEM(gates.shape, f32), dma,
            dma((n_lo,)), dma((n_lo,)),
            dma((layers, chunks)), dma((layers, chunks)),
            dma((chunks, n_lo)), dma((chunks, n_lo)),
            dma((layers,)), dma((layers,)),
            dma((layers, n_hi)), dma((layers, n_hi)),
            dma((layers, n_chip)), dma((layers, n_chip)),
            dma((layers, n_lo)), dma((layers, n_lo)),
            dma,
        ],
        compiler_params=pltpu.CompilerParams(
            collective_id=0, has_side_effects=True, vmem_limit_bytes=56 * 1024 * 1024
        ),
    )(swap_order, as_rows(ket_state), as_rows(bra_state), gates, targets[:, :, None, :])
    return (
        from_rows(ket_out),
        from_rows(bra_out),
        grads.reshape(layers, gate_count, 2, rows, width),
    )


exact_mode = lax.Precision.HIGHEST


def relabel(gate_matrix, ordering):
    gate_width = gate_matrix.shape[-1]
    picker = (ordering[:, None] == jnp.arange(gate_width, dtype=jnp.int32)[None, :]).astype(
        jnp.float32
    )
    return jnp.einsum("ik,ckl,jl->cij", picker, gate_matrix, picker, precision=exact_mode)


def right_apply(amplitudes, gate_matrix):
    real_part = jnp.einsum(
        "...j,ij->...i", amplitudes[0], gate_matrix[0], precision=exact_mode
    ) - jnp.einsum("...j,ij->...i", amplitudes[1], gate_matrix[1], precision=exact_mode)
    imag_part = jnp.einsum(
        "...j,ij->...i", amplitudes[0], gate_matrix[1], precision=exact_mode
    ) + jnp.einsum("...j,ij->...i", amplitudes[1], gate_matrix[0], precision=exact_mode)
    return jnp.stack([real_part, imag_part])


def left_apply(amplitudes, gate_matrix):
    real_part = jnp.einsum(
        "ij,djr->dir", gate_matrix[0], amplitudes[0], precision=exact_mode
    ) - jnp.einsum("ij,djr->dir", gate_matrix[1], amplitudes[1], precision=exact_mode)
    imag_part = jnp.einsum(
        "ij,djr->dir", gate_matrix[1], amplitudes[0], precision=exact_mode
    ) + jnp.einsum("ij,djr->dir", gate_matrix[0], amplitudes[1], precision=exact_mode)
    return jnp.stack([real_part, imag_part])


def low_grad(bra_view, ket_view):
    real_part = jnp.einsum(
        "ri,rj->ij", bra_view[0], ket_view[0], precision=exact_mode
    ) + jnp.einsum("ri,rj->ij", bra_view[1], ket_view[1], precision=exact_mode)
    imag_part = jnp.einsum(
        "ri,rj->ij", bra_view[1], ket_view[0], precision=exact_mode
    ) - jnp.einsum("ri,rj->ij", bra_view[0], ket_view[1], precision=exact_mode)
    return jnp.stack([real_part, imag_part])


def high_grad(bra_view, ket_view):
    real_part = jnp.einsum(
        "dir,djr->ij", bra_view[0], ket_view[0], precision=exact_mode
    ) + jnp.einsum("dir,djr->ij", bra_view[1], ket_view[1], precision=exact_mode)
    imag_part = jnp.einsum(
        "dir,djr->ij", bra_view[1], ket_view[0], precision=exact_mode
    ) - jnp.einsum("dir,djr->ij", bra_view[0], ket_view[1], precision=exact_mode)
    return jnp.stack([real_part, imag_part])


def advance(ket_state, bra_state, gate_matrix, kind, devices):
    gate_width = gate_matrix.shape[-1]
    if kind == 0:
        ket_view = ket_state.reshape(2, -1, gate_width)
        bra_view = bra_state.reshape(2, -1, gate_width)
        ket_next = right_apply(ket_view, gate_matrix)
        gradient = low_grad(bra_view, ket_next)
        bra_next = right_apply(bra_view, gate_matrix)
    else:
        ket_view = ket_state.reshape(2, devices, gate_width, -1)
        bra_view = bra_state.reshape(2, devices, gate_width, -1)
        ket_next = left_apply(ket_view, gate_matrix)
        gradient = high_grad(bra_view, ket_next)
        bra_next = left_apply(bra_view, gate_matrix)
    return (ket_next.reshape(ket_state.shape), bra_next.reshape(bra_state.shape), gradient)


def swap_states(ket_state, bra_state, ordering, block_count):
    outgoing = (
        jnp.take(ket_state.reshape(2, block_count, -1), ordering, axis=1),
        jnp.take(bra_state.reshape(2, block_count, -1), ordering, axis=1),
    )
    ket_incoming, bra_incoming = (
        lax.all_to_all(outgoing[0], "lo", split_axis=1, concat_axis=1, tiled=True),
        lax.all_to_all(outgoing[1], "lo", split_axis=1, concat_axis=1, tiled=True),
    )
    return (ket_incoming.reshape(ket_state.shape), bra_incoming.reshape(bra_state.shape))


def swap_with_gate(ket_state, bra_state, ordering, gate_matrix, block_count):
    gate_width = gate_matrix.shape[-1]
    ket_outgoing = jnp.take(ket_state.reshape(2, block_count, -1), ordering, axis=1).reshape(
        2, block_count, -1, gate_width
    )
    bra_outgoing = jnp.take(bra_state.reshape(2, block_count, -1), ordering, axis=1).reshape(
        2, block_count, -1, gate_width
    )
    ket_piece = lax.all_to_all(ket_outgoing, "lo", split_axis=1, concat_axis=1, tiled=True)
    bra_piece = lax.all_to_all(bra_outgoing, "lo", split_axis=1, concat_axis=1, tiled=True)
    return (right_apply(ket_piece, gate_matrix), bra_piece, right_apply(bra_piece, gate_matrix))


def body(ket_state, bra_state, gates, targets, swap_order):
    gate_width = gates.shape[-1]
    layer_count = gates.shape[0]
    gate_count = gates.shape[1]
    block_count = lax.axis_size("lo")
    group_count = lax.axis_size("hi")
    amp_count = ket_state.shape[1]
    grad_scale = (amp_count * block_count * group_count // gate_width) ** (-0.5)
    row_count = gate_width // group_count
    collected = []
    carried = None
    for layer_index in range(layer_count):
        gradients = []
        for gate_index in range(gate_count):
            if carried is not None and gate_index == 0:
                ket_arrived, bra_before, bra_arrived = carried
                gradient = low_grad(
                    bra_before.reshape(2, -1, gate_width), ket_arrived.reshape(2, -1, gate_width)
                )
                ket_state = ket_arrived.reshape(2, amp_count)
                bra_state = bra_arrived.reshape(2, amp_count)
                carried = None
            else:
                gate_matrix = relabel(
                    gates[layer_index, gate_index], targets[layer_index, gate_index]
                )
                ket_state, bra_state, gradient = advance(
                    ket_state, bra_state, gate_matrix, gate_index % 2, 1
                )
            gradients.append(gradient * grad_scale)
        stacked = jnp.stack(gradients)
        summed = lax.psum(stacked, ("hi", "lo"))
        collected.append(
            lax.dynamic_slice_in_dim(summed, lax.axis_index("hi") * row_count, row_count, 2)
        )
        if layer_index + 1 < layer_count:
            next_gate = relabel(gates[layer_index + 1, 0], targets[layer_index + 1, 0])
            carried = swap_with_gate(
                ket_state, bra_state, swap_order[layer_index], next_gate, block_count
            )
        else:
            ket_state, bra_state = swap_states(
                ket_state, bra_state, swap_order[layer_index], block_count
            )
    all_grads = jnp.stack(collected)
    return (ket_state, bra_state, all_grads)


def solution(mesh):
    specs = dict(
        mesh=mesh,
        in_specs=(P(None, ("hi", "lo")), P(None, ("hi", "lo")), P(), P(), P()),
        out_specs=(P(None, ("hi", "lo")), P(None, ("hi", "lo")), P(None, None, None, "hi", None)),
        check_vma=False,
    )

    def run(ket_state, bra_state, gates, targets, swap_order):
        n_hi, n_lo = mesh.shape["hi"], mesh.shape["lo"]
        _, gate_count, _, width, _ = gates.shape
        chunks = ket_state.shape[1] // (n_hi * n_lo * width * width)
        fits = (
            width % (8 * n_lo) == 0
            and n_lo % 2 == 0
            and width % (4 * n_hi * n_lo) == 0
            and gate_count % 2 == 0
            and chunks == n_lo // 2
            and gates.shape[0] >= 4
        )
        chosen = fast_body if fits else body
        return jax.shard_map(chosen, **specs)(ket_state, bra_state, gates, targets, swap_order)

    return run
```

profile of v0, /device:TPU:0, one launch (start us, length us, event | category | flops | bytes accessed | tf_op | source)
XLA Modules:
  0.0 68.7 jit_solution(13250195083078279712)
XLA Ops:
  0.6 63.4 %shard_map.76 = (f32[1024,128]{1,0:T(8,128)}, f32[1024,128]{1,0:T(8,128)}, f32[4,4,2,4,8,128]{5,4,3,2,1,0:T(8,128)}) custom-call(s32[4,8]{1,0:T(4,128)} %sigma_ref.1, f32[1024,128]{1,0:T(8,128)} %bitcast.25, f32[1024,128]{1,0:T(8,128)} %bitcast.26, f32[4,4,2,128,128]{4,3,2,1,0:T(8,128)} %gates_hbm.1, s32[4,4,1,128]{3,2,1,0:T(1,128)} %bitcast.27), custom_call_target="tpu_custom_call" | custom-call | tf_op jit(solution)/shard_map/pallas_call | solution.py:399
  64.1 0.0 copy-start
  64.1 1.9 %copy.15 = f32[2,65536]{1,0:T(2,128)} copy(f32[2,65536]{1,0:T(2,128)} %bitcast.24) | data formatting | bytes 1048576
  66.0 1.9 %copy.16 = f32[2,65536]{1,0:T(2,128)} copy(f32[2,65536]{1,0:T(2,128)} %bitcast.23) | data formatting | bytes 1048576
  67.9 0.0 copy-done
  67.9 0.8 %copy.17 = f32[4,4,2,32,128]{4,3,2,1,0:T(8,128)} copy(f32[4,4,2,32,128]{4,3,2,1,0:T(8,128)S(1)} %bitcast.22) | data formatting | bytes 1048576
Async XLA Ops:
  64.1 3.8 %copy-start = (f32[4,4,2,4,8,128]{5,4,3,2,1,0:T(8,128)S(1)}, f32[4,4,2,4,8,128]{5,4,3,2,1,0:T(8,128)}, u32[]{:S(2)}) copy-start(f32[4,4,2,4,8,128]{5,4,3,2,1,0:T(8,128)} %get-tuple-element.8) | copy-start | bytes 1572868
where the time goes:
time: 68.9 us; the launch traced here: 68.7 us
  Pallas kernels  63.4 us (92%)
  local copies, waits for them, and re-layouts  4.59 us (7%)
    pallas_call x1, Pallas kernels, fast_body(): pl.pallas_call(functools.partial(kernel, n_hi, n_lo, layers, gate_count,...  63.4 us
    unnamed x5, local copies, waits for them, and re-layouts  4.59 us

commit v1 on v0

--- a/solution.py
+++ b/solution.py
@@ -37,9 +37,11 @@
 
 def kernel(
     n_hi, n_lo, layers, gate_count, chunks, width, scale,
-    sigma_ref, ket_ref, bra_ref, gates_hbm, targets_ref, ket_out, bra_out, grad_hbm,
-    rbuf, sbuf, ybuf, vbuf, acc, r0buf, hsum, r1buf, p1, r2buf, gout,
-    gates_ref, gates_sem, gather_s, gather_r, trade_s, trade_r, home_s, home_r, s0, q0, s1, q1, s2, q2, s3, q3, gsem,
+    sigma_ref, ket_hbm, bra_hbm, gates_hbm, targets_ref, ket_out, bra_out, grad_hbm,
+    ket_ref, bra_ref, rbuf, sbuf, ybuf, vbuf, tape_b, tape_even, tape_odd,
+    acc, r0buf, hsum, r1buf, p1, r2buf, x1buf, x2, x2buf, gout,
+    gates_ref, in_sem, out_sem, gather_s, gather_r, trade_s, trade_r, home_s, home_r,
+    s0, q0, s1, q1, s2, q2, s3, q3,
 ):
     h = lax.axis_index("hi")
     q = lax.axis_index("lo")
@@ -49,6 +51,8 @@
     half = gate_count // 2
     rows = width // n_hi
     piece = rows // n_chip
+    w2 = 2 * width
+    last = layers - 1
 
     def lo_peer(k):
         return lax.rem(q + k, n_lo)
@@ -57,10 +61,29 @@
         return lax.rem(h + k, n_hi)
 
     def chip_peer(k):
-        return lax.rem(chip + k, n_chip)
-
-    gates_copy = pltpu.make_async_copy(gates_hbm, gates_ref, gates_sem)
-    gates_copy.start()
+        peer, bit = 0, 1
+        while bit < n_chip:
+            own = lax.rem(chip // bit, 2)
+            peer = peer + bit * (1 - own if k & bit else own)
+            bit *= 2
+        return peer
+
+    in_copies = [
+        pltpu.make_async_copy(gates_hbm.at[0], gates_ref.at[0], in_sem.at[0]),
+        pltpu.make_async_copy(ket_hbm, ket_ref, in_sem.at[1]),
+        pltpu.make_async_copy(bra_hbm, bra_ref, in_sem.at[2]),
+        pltpu.make_async_copy(
+            gates_hbm.at[pl.ds(1, last)], gates_ref.at[pl.ds(1, last)], in_sem.at[3]
+        ),
+    ]
+    for copy in in_copies:
+        copy.start()
+
+    barrier = pltpu.get_barrier_semaphore()
+    for k in range(1, n_lo):
+        pl.semaphore_signal(barrier, inc=1, device_id={"lo": lo_peer(k)})
+    for k in range(1, n_hi):
+        pl.semaphore_signal(barrier, inc=1, device_id={"hi": hi_peer(k)})
 
     def entering(m):
         parts = [
@@ -70,12 +93,6 @@
             for c in range(2)
         ]
         return jnp.concatenate(parts, axis=0)
-
-    barrier = pltpu.get_barrier_semaphore()
-    for k in range(1, n_lo):
-        pl.semaphore_signal(barrier, inc=1, device_id={"lo": lo_peer(k)})
-    for k in range(1, n_hi):
-        pl.semaphore_signal(barrier, inc=1, device_id={"hi": hi_peer(k)})
 
     def prepare(layer, gate):
         order = targets_ref[layer, gate]
@@ -101,20 +118,19 @@
             axis=0,
         )
 
-    gates_copy.wait()
-    for g in range(gate_count):
-        prepare(0, g)
-    acc[...] = jnp.zeros_like(acc)
-    pl.semaphore_wait(barrier, n_lo - 1 + n_hi - 1)
-
-    def gather_copy(kc, ke, incoming=False):
+    chip_order = list(range(n_chip - 1, -1, -1))
+    targets_order = [(kc, ke) for kc in chip_order for ke in (1, 0)]
+    others = [pair for pair in targets_order if pair != (0, 0)]
+    part = chunks // 2
+
+    def gather_copy(kc, ke, p, incoming=False):
         m, e = chip_peer(kc), lax.rem(core + ke, 2)
         d = 2 * m + e
         return pltpu.make_async_remote_copy(
-            src_ref=sbuf.at[0, m, pl.ds(chunks * e, chunks)],
-            dst_ref=rbuf.at[1, :, :, d if incoming else q],
-            send_sem=gather_s.at[d],
-            recv_sem=gather_r.at[d if incoming else q],
+            src_ref=sbuf.at[0, m, pl.ds(chunks * e + part * p, part)],
+            dst_ref=rbuf.at[1, pl.ds(part * p, part), :, d if incoming else q],
+            send_sem=gather_s.at[p, d],
+            recv_sem=gather_r.at[p, d if incoming else q],
             device_id={"lo": d},
         )
 
@@ -138,11 +154,6 @@
             device_id={"lo": d},
         )
 
-    last = layers - 1
-    chip_order = [k for k in range(n_chip) if k % 2] + list(range(2, n_chip, 2)) + [0]
-    targets_order = [(kc, ke) for kc in chip_order for ke in (1, 0)]
-    others = [pair for pair in targets_order if pair != (0, 0)]
-
     def r0_copy(l):
         return pltpu.make_async_remote_copy(
             src_ref=acc.at[l, pl.ds(half * (1 - core), half)],
@@ -152,21 +163,31 @@
             device_id={"lo": q + 1 - 2 * core},
         )
 
-    def r1_copy(l, k, incoming=False):
+    lo_first = (1,)
+
+    def hi_copy(l, k, incoming=False):
         d = hi_peer(k)
+        if l in lo_first:
+            src, dst = x2.at[l, :, :, d], x2buf.at[l, d if incoming else h]
+        else:
+            src, dst = hsum.at[l, :, :, d], r1buf.at[l, d if incoming else h]
         return pltpu.make_async_remote_copy(
-            src_ref=hsum.at[l, :, :, d],
-            dst_ref=r1buf.at[l, d if incoming else h],
+            src_ref=src,
+            dst_ref=dst,
             send_sem=s1.at[l, d],
             recv_sem=q1.at[l, d if incoming else h],
             device_id={"hi": d},
         )
 
-    def r2_copy(l, k, incoming=False):
+    def chip_copy(l, k, incoming=False):
         d = chip_peer(k)
+        if l in lo_first:
+            src, dst = hsum.at[l, :, :, :, d], x1buf.at[l, d if incoming else chip]
+        else:
+            src, dst = p1.at[l, :, :, d], r2buf.at[l, d if incoming else chip]
         return pltpu.make_async_remote_copy(
-            src_ref=p1.at[l, :, :, d],
-            dst_ref=r2buf.at[l, d if incoming else chip],
+            src_ref=src,
+            dst_ref=dst,
             send_sem=s2.at[l, d],
             recv_sem=q2.at[l, d if incoming else chip],
             device_id={"lo": 2 * d + core},
@@ -184,38 +205,69 @@
             device_id={"lo": d},
         )
 
+    def hi_start(l):
+        for k in range(n_hi - 1, 0, -1):
+            hi_copy(l, k).start()
+
+    def chip_start(l):
+        for k in range(n_chip - 1, 0, -1):
+            chip_copy(l, k).start()
+
     def stage0(l):
         r0_copy(l).wait_recv()
         total = acc[l, pl.ds(half * core, half)] + r0buf[l]
-        hsum[l] = total.reshape(half, 2, n_hi, rows, width)
-        for k in range(1, n_hi):
-            r1_copy(l, k).start()
+        hsum[l] = total.reshape(half, 2, n_hi, n_chip, piece, width)
+        if l in lo_first:
+            chip_start(l)
+        else:
+            hi_start(l)
 
     def stage1(l):
-        total = hsum[l, :, :, h]
-        for k in range(1, n_hi):
-            r1_copy(l, k, True).wait_recv()
-            total = total + r1buf[l, hi_peer(k)]
-        p1[l] = total.reshape(half, 2, n_chip, piece, width)
-        for k in range(1, n_chip):
-            r2_copy(l, k).start()
+        if l in lo_first:
+            total = hsum[l, :, :, :, chip]
+            for k in range(1, n_chip):
+                chip_copy(l, k, True).wait_recv()
+                total = total + x1buf[l, chip_peer(k)]
+            x2[l] = total
+            hi_start(l)
+        else:
+            total = hsum[l, :, :, h]
+            for k in range(1, n_hi):
+                hi_copy(l, k, True).wait_recv()
+                total = total + r1buf[l, hi_peer(k)]
+            p1[l] = total
+            chip_start(l)
 
     def stage2(l):
-        total = p1[l, :, :, chip]
-        for k in range(1, n_chip):
-            r2_copy(l, k, True).wait_recv()
-            total = total + r2buf[l, chip_peer(k)]
+        if l in lo_first:
+            total = x2[l, :, :, h]
+            for k in range(1, n_hi):
+                hi_copy(l, k, True).wait_recv()
+                total = total + x2buf[l, hi_peer(k)]
+        else:
+            total = p1[l, :, :, chip]
+            for k in range(1, n_chip):
+                chip_copy(l, k, True).wait_recv()
+                total = total + r2buf[l, chip_peer(k)]
         gout[l, pl.ds(half * core, half), :, chip] = total * scale
+        for k in range(n_lo - 1, 0, -1):
+            r3_copy(l, k).start()
+
+    def grad_out(l):
+        return pltpu.make_async_copy(gout.at[l], grad_hbm.at[l], out_sem.at[2 + l])
+
+    def stage3(l):
         for k in range(1, n_lo):
-            r3_copy(l, k).start()
+            r3_copy(l, k, True).wait_recv()
+        grad_out(l).start()
 
     def cat(v, axis):
         return jnp.concatenate(v, axis=axis) if len(v) > 1 else v[0]
 
-    def run_gates(ss, l):
+    def apply_gates(ss, l, first):
         n = len(ss)
-        w2 = 2 * width
         hs, ls = zip(*[split(s) for s in ss])
+        spans = [slice((first + i) * width, (first + i + 1) * width) for i in range(n)]
         for g in range(gate_count):
             v = vbuf[l, g]
             if g % 2 == 0:
@@ -224,10 +276,12 @@
                 y = mm_nt(cat([xh, xl, xh], 1), v)
                 ys = [y[i * w2:(i + 1) * w2] for i in range(n)]
                 yhs, yls = zip(*[split(t) for t in ys])
-                bt = cat([cat([s[:width, width:], s[width:, width:]], 1).T for s in ss], 1)
-                bh, bl = split(bt)
-                kh, kl = cat([t[:width] for t in yhs], 0), cat([t[:width] for t in yls], 0)
-                grad = mm(cat([bh, bh, bl], 1), cat([kh, kl, kh], 0))
+                for s, yh, yl, span in zip(ss, yhs, yls, spans):
+                    bh, bl = split(cat([s[:width, width:], s[width:, width:]], 1).T)
+                    tape_b[g, 0, :, span] = bh
+                    tape_b[g, 1, :, span] = bl
+                    tape_even[g // 2, 0, span, :] = yh[:width]
+                    tape_even[g // 2, 1, span, :] = yl[:width]
                 ss = [block_swap(t) for t in ys]
                 hs = [block_swap(t) for t in yhs]
                 ls = [block_swap(t) for t in yls]
@@ -236,80 +290,105 @@
                 y = mm(v, cat([sh, sl, sh], 0))
                 ys = [y[:, i * w2:(i + 1) * w2] for i in range(n)]
                 yhs, yls = zip(*[split(t) for t in ys])
-                bh, bl = cat([t[:, width:] for t in hs], 1), cat([t[:, width:] for t in ls], 1)
-                kh, kl = cat([t[:, :width] for t in yhs], 1), cat([t[:, :width] for t in yls], 1)
-                grad = mm_nt(cat([bh, bh, bl], 1), cat([kh, kl, kh], 1))
+                for sh, sl, yh, yl, span in zip(hs, ls, yhs, yls, spans):
+                    tape_b[g, 0, :, span] = sh[:, width:]
+                    tape_b[g, 1, :, span] = sl[:, width:]
+                    tape_odd[g // 2, 0, :, span] = yh[:, :width]
+                    tape_odd[g // 2, 1, :, span] = yl[:, :width]
                 ss, hs, ls = ys, yhs, yls
-            acc[l, g, 0] += grad[:width, :width] + grad[width:, width:]
-            acc[l, g, 1] += grad[width:, :width] - grad[:width, width:]
         return ss
 
+    def gradients(l):
+        @pl.loop(0, half)
+        def _(pair):
+            for odd in range(2):
+                g = 2 * pair + odd
+                bh, bl = tape_b[g, 0], tape_b[g, 1]
+                b = cat([bh, bh, bl], 1)
+                if odd:
+                    kh, kl = tape_odd[pair, 0], tape_odd[pair, 1]
+                    grad = mm_nt(b, cat([kh, kl, kh], 1))
+                else:
+                    kh, kl = tape_even[pair, 0], tape_even[pair, 1]
+                    grad = mm(b, cat([kh, kl, kh], 0))
+                acc[l, g, 0] = grad[:width, :width] + grad[width:, width:]
+                acc[l, g, 1] = grad[width:, :width] - grad[:width, width:]
+
+        r0_copy(l).start()
+
     def load(l, i):
-        return rbuf[l, i].reshape(2 * width, 2 * width)
-
-    for first in range(0, chunks, 2):
-        todo = chip_order[first:first + 2]
-        states = run_gates([entering(chip_peer(kc)) for kc in todo], 0)
+        return rbuf[l, i].reshape(w2, w2)
+
+    in_copies[0].wait()
+    for g in range(gate_count):
+        prepare(0, g)
+    in_copies[1].wait()
+    in_copies[2].wait()
+    done = 0
+    for todo in (chip_order[:1], chip_order[1:]):
+        states = apply_gates([entering(chip_peer(kc)) for kc in todo], 0, done)
+        done += len(todo)
         for kc, state in zip(todo, states):
-            m = chip_peer(kc)
             ybuf[kc] = state.reshape(ybuf.shape[1:])
-            for ke in (1, 0):
-                e = lax.rem(core + ke, 2)
+        if todo[0] == chip_order[0]:
+            pl.semaphore_wait(barrier, n_lo - 1 + n_hi - 1)
+        for p in range(2):
+            for kc in todo:
+                m = chip_peer(kc)
+                for ke in (1, 0):
+                    e = lax.rem(core + ke, 2)
+                    for j in range(part * p, part * (p + 1)):
+                        block = ybuf[kc, :, sigma_ref[0, 2 * j + e]]
+                        if (kc, ke) == (0, 0):
+                            rbuf[1, j, :, q] = block
+                        else:
+                            sbuf[0, m, chunks * e + j] = block
+                    if (kc, ke) != (0, 0):
+                        gather_copy(kc, ke, p).start()
+    gradients(0)
+    in_copies[3].wait()
+
+    def prepare_layers(first, end):
+        @pl.loop(first, end)
+        def _(l):
+            for g in range(gate_count):
+                prepare(l, g)
+
+    prepare_layers(1, 2)
+    stage0(0)
+    prepare_layers(2, layers)
+
+    for l in range(1, last):
+        for p in range(2):
+            if l == 1:
+                for kc, ke in others:
+                    gather_copy(kc, ke, p, True).wait_recv()
+            elif p == 0:
+                for i in range(chunks):
+                    trade_copy(l - 1, i, True).wait_recv()
+            todo = range(part * p, part * (p + 1))
+            states = apply_gates([load(l, i) for i in todo], l, part * p)
+            for i, state in zip(todo, states):
+                ybuf[i] = state.reshape(ybuf.shape[1:])
                 for j in range(chunks):
-                    block = ybuf[kc, :, sigma_ref[0, 2 * j + e]]
-                    if (kc, ke) == (0, 0):
-                        rbuf[1, j, :, q] = block
-                    else:
-                        sbuf[0, m, chunks * e + j] = block
-                if (kc, ke) != (0, 0):
-                    gather_copy(kc, ke).start()
-    r0_copy(0).start()
-
-    @pl.loop(1, layers)
-    def _(l):
-        @pl.loop(0, gate_count)
-        def _(g):
-            prepare(l, g)
-
-    stage0(0)
-    for kc, ke in others:
-        gather_copy(kc, ke, True).wait_recv()
-
-    def middle(l):
-        states = run_gates([load(l, i) for i in range(chunks)], l)
-        for i, state in enumerate(states):
-            ybuf[i] = state.reshape(ybuf.shape[1:])
-            for j in range(chunks):
-                sbuf[l, i, j] = ybuf[i, :, sigma_ref[l, 2 * j + 1 - core]]
-            trade_copy(l, i).start()
-            for j in range(chunks):
-                rbuf[l + 1, j, :, 2 * i + core] = ybuf[i, :, sigma_ref[l, 2 * j + core]]
-        r0_copy(l).start()
-
-    @pl.loop(1, last)
-    def _(l):
-        middle(l)
-
-        @pl.when(l == 1)
-        def _():
+                    sbuf[l, i, j] = ybuf[i, :, sigma_ref[l, 2 * j + 1 - core]]
+                trade_copy(l, i).start()
+                for j in range(chunks):
+                    rbuf[l + 1, j, :, 2 * i + core] = ybuf[i, :, sigma_ref[l, 2 * j + core]]
+            if l > 1 and p == 0:
+                stage0(l - 1)
+        if l == 1:
             stage1(0)
-
-        @pl.when(l > 2)
-        def _():
-            stage1(l - 2)
-
-        @pl.when(l > 1)
-        def _():
+        else:
             stage2(l - 2)
-            stage0(l - 1)
-
-        for i in range(chunks):
-            trade_copy(l, i, True).wait_recv()
-
-    for first in range(0, chunks, 2):
-        states = run_gates([load(last, first + i) for i in range(2)], last)
-        for i, state in enumerate(states):
-            i = first + i
+            stage1(l - 1)
+        gradients(l)
+
+    for i in range(chunks):
+        trade_copy(last - 1, i, True).wait_recv()
+    for todo in ([0], range(1, chunks)):
+        states = apply_gates([load(last, i) for i in todo], last, todo[0])
+        for i, state in zip(todo, states):
             ybuf[i] = state.reshape(ybuf.shape[1:])
             for kc, ke in targets_order:
                 d = 2 * chip_peer(kc) + lax.rem(core + ke, 2)
@@ -319,16 +398,14 @@
                 else:
                     sbuf[last, i, d] = block
                     home_copy(i, kc, ke).start()
-        if first == 0:
+        if todo[0] == 0:
             stage0(last - 1)
-    r0_copy(last).start()
-    stage1(last - 2)
+    gradients(last)
+    stage2(last - 2)
     stage0(last)
     stage1(last - 1)
-    stage2(last - 2)
-    stage1(last)
-    stage2(last - 1)
-    stage2(last)
+    for l in range(last - 2):
+        stage3(l)
 
     for kc in [0] + [k for k in chip_order if k]:
         for ke in (1, 0):
@@ -338,21 +415,26 @@
         m = chip_peer(kc)
         state = load(layers, m)
         for c in range(2):
-            for n, out in enumerate((ket_out, bra_out)):
+            for n, out in enumerate((ket_ref, bra_ref)):
                 out[pl.ds(2 * m + c, width, stride=2 * chunks), :] = state[
                     c * width:(c + 1) * width, n * width:(n + 1) * width
                 ]
-
-    @pl.loop(0, layers)
-    def _(l):
-        for k in range(1, n_lo):
-            r3_copy(l, k, True).wait_recv()
-
-    grads = pltpu.make_async_copy(gout, grad_hbm, gsem)
-    grads.start()
+    state_out = [
+        pltpu.make_async_copy(ket_ref, ket_out, out_sem.at[0]),
+        pltpu.make_async_copy(bra_ref, bra_out, out_sem.at[1]),
+    ]
+    for copy in state_out:
+        copy.start()
+
+    stage1(last)
+    stage2(last - 1)
+    stage2(last)
+    for l in range(last - 2, layers):
+        stage3(l)
 
     for kc, ke in others:
-        gather_copy(kc, ke).wait_send()
+        for p in range(2):
+            gather_copy(kc, ke, p).wait_send()
 
     @pl.loop(0, chunks)
     def _(i):
@@ -363,17 +445,19 @@
         def _(l):
             trade_copy(l, i).wait_send()
 
-    @pl.loop(0, layers)
-    def _(l):
+    for l in range(layers):
         r0_copy(l).wait_send()
         for k in range(1, n_hi):
-            r1_copy(l, k).wait_send()
+            hi_copy(l, k).wait_send()
         for k in range(1, n_chip):
-            r2_copy(l, k).wait_send()
+            chip_copy(l, k).wait_send()
         for k in range(1, n_lo):
             r3_copy(l, k).wait_send()
 
-    grads.wait()
+    for copy in state_out:
+        copy.wait()
+    for l in range(layers):
+        grad_out(l).wait()
 
 
 def fast_body(ket_state, bra_state, gates, targets, swap_order):
@@ -388,6 +472,7 @@
     piece = rows // n_chip
     scale = (amps * n_lo * n_hi // width) ** (-0.5)
     shape = (chunks, 2, n_lo, unit, 2 * width)
+    flat = (2 * amps // width, width)
 
     def as_rows(v):
         return v.reshape(2, amps // width, width).transpose(1, 0, 2).reshape(-1, width)
@@ -399,43 +484,47 @@
     ket_out, bra_out, grads = pl.pallas_call(
         functools.partial(kernel, n_hi, n_lo, layers, gate_count, chunks, width, scale),
         out_shape=(
-            jax.ShapeDtypeStruct((2 * amps // width, width), f32),
-            jax.ShapeDtypeStruct((2 * amps // width, width), f32),
+            jax.ShapeDtypeStruct(flat, f32),
+            jax.ShapeDtypeStruct(flat, f32),
             jax.ShapeDtypeStruct((layers, gate_count, 2, n_chip, piece, width), f32),
         ),
         in_specs=[
             pl.BlockSpec(memory_space=pltpu.SMEM),
-            pl.BlockSpec(memory_space=pltpu.VMEM),
-            pl.BlockSpec(memory_space=pltpu.VMEM),
+            pl.BlockSpec(memory_space=pl.ANY),
+            pl.BlockSpec(memory_space=pl.ANY),
             pl.BlockSpec(memory_space=pl.ANY),
             pl.BlockSpec(memory_space=pltpu.VMEM),
         ],
-        out_specs=[
-            pl.BlockSpec(memory_space=pltpu.VMEM),
-            pl.BlockSpec(memory_space=pltpu.VMEM),
-            pl.BlockSpec(memory_space=pl.ANY),
-        ],
+        out_specs=[pl.BlockSpec(memory_space=pl.ANY)] * 3,
         scratch_shapes=[
+            pltpu.VMEM(flat, f32),
+            pltpu.VMEM(flat, f32),
             pltpu.VMEM((layers + 1,) + shape, f32),
             pltpu.VMEM((layers, chunks, n_lo, 2, unit, 2 * width), f32),
             pltpu.VMEM(shape, f32),
             pltpu.VMEM((layers, gate_count, 2 * width, 6 * width), bf16),
+            pltpu.VMEM((gate_count, 2, 2 * width, chunks * width), bf16),
+            pltpu.VMEM((half, 2, chunks * width, 2 * width), bf16),
+            pltpu.VMEM((half, 2, 2 * width, chunks * width), bf16),
             pltpu.VMEM((layers, gate_count, 2, width, width), f32),
             pltpu.VMEM((layers, half, 2, width, width), f32),
-            pltpu.VMEM((layers, half, 2, n_hi, rows, width), f32),
-            pltpu.VMEM((layers, n_hi, half, 2, rows, width), f32),
+            pltpu.VMEM((layers, half, 2, n_hi, n_chip, piece, width), f32),
+            pltpu.VMEM((layers, n_hi, half, 2, n_chip, piece, width), f32),
             pltpu.VMEM((layers, half, 2, n_chip, piece, width), f32),
             pltpu.VMEM((layers, n_chip, half, 2, piece, width), f32),
+            pltpu.VMEM((layers, n_chip, half, 2, n_hi, piece, width), f32),
+            pltpu.VMEM((layers, half, 2, n_hi, piece, width), f32),
+            pltpu.VMEM((layers, n_hi, half, 2, piece, width), f32),
             pltpu.VMEM((layers, gate_count, 2, n_chip, piece, width), f32),
-            pltpu.VMEM(gates.shape, f32), dma,
-            dma((n_lo,)), dma((n_lo,)),
+            pltpu.VMEM(gates.shape, f32),
+            dma((4,)), dma((2 + layers,)),
+            dma((2, n_lo)), dma((2, n_lo)),
             dma((layers, chunks)), dma((layers, chunks)),
             dma((chunks, n_lo)), dma((chunks, n_lo)),
             dma((layers,)), dma((layers,)),
             dma((layers, n_hi)), dma((layers, n_hi)),
             dma((layers, n_chip)), dma((layers, n_chip)),
             dma((layers, n_lo)), dma((layers, n_lo)),
-            dma,
         ],
         compiler_params=pltpu.CompilerParams(
             collective_id=0, has_side_effects=True, vmem_limit_bytes=56 * 1024 * 1024
@@ -607,6 +696,7 @@
             and width % (4 * n_hi * n_lo) == 0
             and gate_count % 2 == 0
             and chunks == n_lo // 2
+            and chunks in (4, 8, 16)
             and gates.shape[0] >= 4
         )
         chosen = fast_body if fits else body

time: 68.9 us -> 63.1 us (0.916)
  Pallas kernels: 63.4 us -> 57.7 us
    pallas_call x1, Pallas kernels: 63.4 us -> 57.7 us  [fast_body(): pl.pallas_call(functools.partial(kernel, n_hi, n_lo, layers, gate_count,...]
where the time goes in v1:
time: 63.1 us; the launch traced here: 62.9 us
  Pallas kernels  57.7 us (91%)
  local copies, waits for them, and re-layouts  4.59 us (7%)
  between operations  0.65 us (1%)
    pallas_call x1, Pallas kernels, fast_body(): pl.pallas_call(functools.partial(kernel, n_hi, n_lo, layers, gate_count,...  57.7 us
    unnamed x5, local copies, waits for them, and re-layouts  4.59 us

profile of v1, /device:TPU:0, one launch (start us, length us, event | category | flops | bytes accessed | tf_op | source)
XLA Modules:
  0.0 62.9 jit_solution(2684778871532875130)
XLA Ops:
  0.6 57.7 %shard_map.76 = (f32[1024,128]{1,0:T(8,128)}, f32[1024,128]{1,0:T(8,128)}, f32[4,4,2,4,8,128]{5,4,3,2,1,0:T(8,128)}) custom-call(s32[4,8]{1,0:T(4,128)} %sigma_ref.1, f32[1024,128]{1,0:T(8,128)} %bitcast.25, f32[1024,128]{1,0:T(8,128)} %bitcast.26, f32[4,4,2,128,128]{4,3,2,1,0:T(8,128)} %gates_hbm.1, s32[4,4,1,128]{3,2,1,0:T(1,128)} %bitcast.27), custom_call_target="tpu_custom_call" | custom-call | tf_op jit(solution)/shard_map/pallas_call | solution.py:484
  58.3 0.0 copy-start
  58.3 1.9 %copy.15 = f32[2,65536]{1,0:T(2,128)} copy(f32[2,65536]{1,0:T(2,128)} %bitcast.24) | data formatting | bytes 1048576
  60.2 1.9 %copy.16 = f32[2,65536]{1,0:T(2,128)} copy(f32[2,65536]{1,0:T(2,128)} %bitcast.23) | data formatting | bytes 1048576
  62.1 0.0 copy-done
  62.1 0.8 %copy.17 = f32[4,4,2,32,128]{4,3,2,1,0:T(8,128)} copy(f32[4,4,2,32,128]{4,3,2,1,0:T(8,128)S(1)} %bitcast.22) | data formatting | bytes 1048576
Async XLA Ops:
  58.3 3.8 %copy-start = (f32[4,4,2,4,8,128]{5,4,3,2,1,0:T(8,128)S(1)}, f32[4,4,2,4,8,128]{5,4,3,2,1,0:T(8,128)}, u32[]{:S(2)}) copy-start(f32[4,4,2,4,8,128]{5,4,3,2,1,0:T(8,128)} %get-tuple-element.8) | copy-start | bytes 1572868

commit v2 on v1

--- a/solution.py
+++ b/solution.py
@@ -381,8 +381,11 @@
             stage1(0)
         else:
             stage2(l - 2)
+            if l - 1 not in lo_first:
+                stage1(l - 1)
+        gradients(l)
+        if l > 1 and l - 1 in lo_first and l + 1 < last:
             stage1(l - 1)
-        gradients(l)
 
     for i in range(chunks):
         trade_copy(last - 1, i, True).wait_recv()
@@ -401,8 +404,10 @@
         if todo[0] == 0:
             stage0(last - 1)
     gradients(last)
+    if last - 2 in lo_first:
+        stage1(last - 2)
+    stage0(last)
     stage2(last - 2)
-    stage0(last)
     stage1(last - 1)
     for l in range(last - 2):
         stage3(l)
@@ -415,17 +420,10 @@
         m = chip_peer(kc)
         state = load(layers, m)
         for c in range(2):
-            for n, out in enumerate((ket_ref, bra_ref)):
+            for n, out in enumerate((ket_out, bra_out)):
                 out[pl.ds(2 * m + c, width, stride=2 * chunks), :] = state[
                     c * width:(c + 1) * width, n * width:(n + 1) * width
                 ]
-    state_out = [
-        pltpu.make_async_copy(ket_ref, ket_out, out_sem.at[0]),
-        pltpu.make_async_copy(bra_ref, bra_out, out_sem.at[1]),
-    ]
-    for copy in state_out:
-        copy.start()
-
     stage1(last)
     stage2(last - 1)
     stage2(last)
@@ -454,10 +452,17 @@
         for k in range(1, n_lo):
             r3_copy(l, k).wait_send()
 
-    for copy in state_out:
-        copy.wait()
     for l in range(layers):
         grad_out(l).wait()
+
+
+def hand_over(ket_in, bra_in, grad_in, ket_out, bra_out, grad_out, put):
+    pairs = ((ket_in, ket_out), (bra_in, bra_out), (grad_in, grad_out))
+    ways = [pltpu.make_async_copy(src, dst, put.at[n]) for n, (src, dst) in enumerate(pairs)]
+    for way in ways:
+        way.start()
+    for way in ways:
+        way.wait()
 
 
 def fast_body(ket_state, bra_state, gates, targets, swap_order):
@@ -484,9 +489,9 @@
     ket_out, bra_out, grads = pl.pallas_call(
         functools.partial(kernel, n_hi, n_lo, layers, gate_count, chunks, width, scale),
         out_shape=(
-            jax.ShapeDtypeStruct(flat, f32),
-            jax.ShapeDtypeStruct(flat, f32),
-            jax.ShapeDtypeStruct((layers, gate_count, 2, n_chip, piece, width), f32),
+            pltpu.VMEM(flat, f32),
+            pltpu.VMEM(flat, f32),
+            pltpu.VMEM((layers, gate_count, 2, n_chip, piece, width), f32),
         ),
         in_specs=[
             pl.BlockSpec(memory_space=pltpu.SMEM),
@@ -495,7 +500,7 @@
             pl.BlockSpec(memory_space=pl.ANY),
             pl.BlockSpec(memory_space=pltpu.VMEM),
         ],
-        out_specs=[pl.BlockSpec(memory_space=pl.ANY)] * 3,
+        out_specs=[pl.BlockSpec(memory_space=pltpu.VMEM)] * 3,
         scratch_shapes=[
             pltpu.VMEM(flat, f32),
             pltpu.VMEM(flat, f32),
@@ -530,6 +535,14 @@
             collective_id=0, has_side_effects=True, vmem_limit_bytes=56 * 1024 * 1024
         ),
     )(swap_order, as_rows(ket_state), as_rows(bra_state), gates, targets[:, :, None, :])
+    ket_out, bra_out, grads = pl.pallas_call(
+        hand_over,
+        out_shape=tuple(jax.ShapeDtypeStruct(v.shape, f32) for v in (ket_out, bra_out, grads)),
+        in_specs=[pl.BlockSpec(memory_space=pltpu.VMEM)] * 3,
+        out_specs=[pl.BlockSpec(memory_space=pl.ANY)] * 3,
+        scratch_shapes=[dma((3,))],
+        compiler_params=pltpu.CompilerParams(vmem_limit_bytes=4 * 1024 * 1024),
+    )(ket_out, bra_out, grads)
     return (
         from_rows(ket_out),
         from_rows(bra_out),

time: 63.1 us -> 57.9 us (0.918)
  local copies, waits for them, and re-layouts: 4.59 us -> 0 us
  Pallas kernels: 57.7 us -> 56.9 us
    unnamed x5 -> x0, local copies, waits for them, and re-layouts: 4.59 us -> none
    pallas_call x1, Pallas kernels: 57.7 us -> 55.7 us  [fast_body(): pl.pallas_call(functools.partial(kernel, n_hi, n_lo, layers, gate_count,...]
    pallas_call x0 -> x1, Pallas kernels: none -> 1.17 us  [fast_body(): pl.pallas_call(hand_over, out_shape=tuple((jax.ShapeDtypeStruct(v.shape,...]
where the time goes in v2:
time: 57.9 us; the launch traced here: 57.7 us
  Pallas kernels  56.9 us (98%)
  between operations  0.8 us (1%)
    pallas_call x1, Pallas kernels, fast_body(): pl.pallas_call(functools.partial(kernel, n_hi, n_lo, layers, gate_count,...  55.7 us
    pallas_call x1, Pallas kernels, fast_body(): pl.pallas_call(hand_over, out_shape=tuple((jax.ShapeDtypeStruct(v.shape,...  1.17 us

profile of v2, /device:TPU:0, one launch (start us, length us, event | category | flops | bytes accessed | tf_op | source)
XLA Modules:
  0.0 57.7 jit_solution(17621419235302451528)
XLA Ops:
  0.6 55.7 %shard_map.76 = (f32[1024,128]{1,0:T(8,128)S(1)}, f32[1024,128]{1,0:T(8,128)S(1)}, f32[4,4,2,4,8,128]{5,4,3,2,1,0:T(8,128)S(1)}) custom-call(s32[4,8]{1,0:T(4,128)} %sigma_ref.1, f32[1024,128]{1,0:T(8,128)} %bitcast.22, f32[1024,128]{1,0:T(8,128)} %bitcast.23, f32[4,4,2,128,128]{4,3,2,1,0:T(8,128)} %gates_hbm.1, s32[4,4,1,128]{3,2,1,0:T(1,128)} %bitcast.24), custom_call_target="tpu_custom_call" | custom-call | tf_op jit(solution)/shard_map/pallas_call | solution.py:489
  56.4 1.2 %shard_map.77 = (f32[1024,128]{1,0:T(8,128)}, f32[1024,128]{1,0:T(8,128)}, f32[4,4,2,4,8,128]{5,4,3,2,1,0:T(8,128)}) custom-call(f32[1024,128]{1,0:T(8,128)S(1)} %get-tuple-element.9.ket_in, f32[1024,128]{1,0:T(8,128)S(1)} %get-tuple-element.10.bra_in, f32[4,4,2,4,8,128]{5,4,3,2,1,0:T(8,128)S(1)} %get-tuple-element.11.grad_in), custom_call_target="tpu_custom_call" | custom-call | tf_op jit(solution)/shard_map/pallas_call | solution.py:538
